TPU v7x, 128 devices: a whole 4x4x4 slice. The times are simulated.
128 devices in a mesh: gx: 4 (over y), gy: 32 (over z, x, core).
Axes of the slice: x: 4, y: 4, z: 4, core: 2. Of those that a mesh axis runs over, the one named last changes fastest.
Arguments:
- patches: bfloat16 [256, 4096, 256], P(('gx', 'gy')), may hold values from -6 to 6
- start_frames: float32 [256, 256, 256], P(('gx', 'gy')), may hold values from -6 to 6
- pair_ends: int32 [1024, 2], P('gx'), may hold values from 0 to 255, as said below
- margin_blocks: int32 [1024, 2, 4], P('gx'), may hold values from 0 to 31, as said below
Outputs:
- aligned: bfloat16 [256, 4096, 256], P(('gx', 'gy'))
- final_frames: float32 [256, 256, 256], P(('gx', 'gy'))
- frame_total: float32 [256, 256], replicated
Inputs may be any that keep to these rules, and one draw needn't show every extreme that they name: `pair_ends`: both ends of a pair lie in the owner's group of 64 patches (patches of the devices with the owner's gx index), on distinct patches; at most 1 ends of one owner's pairs lie on any one device, and ends on one device are of distinct patches; some device holds exactly 1 of some owner's ends. Every patch is an end of some pair. Patch p lives on device p // 2, devices counted with gx slowest. Patch degrees are uneven. `margin_blocks`: the 4 blocks of one end are distinct.
All inputs are finite; a program needn't handle non-finite values.
Results may differ from a plain program's by a relative error of at most 0.012.
The roundings to bfloat16 on the way count: a program that leaves them out, or rounds other values in their place, can miss the bound.
Values may be sent and summed in bfloat16 or wider, within the bound.
No kernel may reach another device: no remote copies, remote signals or barrier semaphores. Data moves between devices by JAX's collectives and lax.ppermute only.
A program may use at most 128 MiB of HBM per device.

v0:
```python
import jax
import jax.numpy as jnp
from jax import lax
from jax.sharding import Mesh
from jax.sharding import PartitionSpec as P

BLOCK = 128
SWEEPS = 2
NS_STEPS = 5
GY = ("gy_0", "gy_1", "gy_2")
GX_GY = ("gx", "gy_0", "gy_1", "gy_2")
coef_first = 3.4445
coef_second = -4.775
coef_third = 2.0315


def rows_for(lines, size):
    spare = -len(lines) % size
    return jnp.pad(lines, [(0, spare)] + [(0, 0)] * (lines.ndim - 1))


def from_everyone(value, axis):
    size = lax.axis_size(axis)
    return lax.all_to_all(
        jnp.broadcast_to(value[None], (size, *value.shape)), axis, 0, 0, tiled=True
    )


def in_order(parts, dim):
    parts = jnp.moveaxis(parts, 0, dim)
    dims = parts.shape
    return parts.reshape(*dims[:dim], dims[dim] * dims[dim + 1], *dims[dim + 2 :])


def whole_of(value, axes, dim):
    far, near = axes
    parts = from_everyone(from_everyone(value, far), near)
    return in_order(parts.swapaxes(0, 1).reshape(-1, *value.shape), dim)


def in_blocks(value, dim, size):
    dims = value.shape
    parts = value.reshape(*dims[:dim], size, dims[dim] // size, *dims[dim + 1 :])
    return jnp.moveaxis(parts, dim, 0)


def sent_and_summed(value, axis, dim):
    parts = in_blocks(value, dim, lax.axis_size(axis))
    arrived = lax.all_to_all(parts, axis, split_axis=0, concat_axis=0, tiled=True)
    return arrived.sum(axis=0)


def sum_by_axis(value, axes, dim):
    far, near = axes
    parts = in_blocks(value, dim, lax.axis_size(far))
    nearer = sent_and_summed(parts, near, dim + 1)
    arrived = lax.all_to_all(nearer, far, split_axis=0, concat_axis=0, tiled=True)
    return arrived.sum(axis=0)


def sum_by_parts(value, axes):
    lines = value.reshape(-1, value.shape[-1])
    padded = rows_for(lines, lax.axis_size(axes[0]) * lax.axis_size(axes[1]))
    whole = whole_of(sum_by_axis(padded, axes, 0), axes, 0)
    return lax.slice_in_dim(whole, 0, len(lines)).reshape(value.shape)


def newton_schulz(matrix):
    scaling = lax.rsqrt(jnp.sum(matrix * matrix, axis=(-2, -1), keepdims=True) + 1e-06)
    matrix = matrix * scaling
    for repeat_index in range(NS_STEPS):
        square = jnp.einsum("...ij,...kj->...ik", matrix, matrix, precision=lax.Precision.HIGHEST)
        polynom = coef_second * square + coef_third * jnp.einsum(
            "...ij,...jk->...ik", square, square, precision=lax.Precision.HIGHEST
        )
        matrix = coef_first * matrix + jnp.einsum(
            "...ij,...jk->...ik", polynom, matrix, precision=lax.Precision.HIGHEST
        )
    return matrix


def local(patches, start_frames, pair_ends, margin_blocks):
    group_size = lax.axis_size(GY)
    my_column = lax.axis_index(GY)
    my_group = lax.axis_index("gx")
    per_device, row_count, width = patches.shape
    pairs_owned = pair_ends.shape[0] // group_size
    ends_count = 2 * pairs_owned
    capacity = -(-ends_count // group_size)
    group_base = my_group * (group_size * per_device)
    local_ids = pair_ends.reshape(group_size, ends_count) - group_base
    partner_ids = pair_ends[:, ::-1].reshape(group_size, ends_count) - group_base
    device_of = local_ids // per_device
    patch_of = local_ids % per_device
    positions = jnp.arange(ends_count, dtype=jnp.int32)
    earlier = positions[None, :] < positions[:, None]
    same_device = device_of[:, :, None] == device_of[:, None, :]
    order_rank = jnp.sum(same_device & earlier[None], axis=2)
    slot_numbers = jnp.arange(capacity, dtype=jnp.int32)
    mine = device_of == my_column
    selected = (mine[:, None, :] & (order_rank[:, None, :] == slot_numbers[None, :, None])).astype(
        jnp.int32
    )
    slot_live = jnp.sum(selected, axis=2)
    slot_patch = jnp.sum(selected * patch_of[:, None, :], axis=2)
    slot_partner = jnp.sum(selected * partner_ids[:, None, :], axis=2)
    blocks_group = margin_blocks.reshape(group_size, ends_count, -1)
    slot_blocks = jnp.sum(selected[:, :, :, None] * blocks_group[:, None, :, :], axis=2)
    offsets = jnp.arange(BLOCK, dtype=jnp.int32)
    row_index = (
        slot_patch[:, :, None, None] * row_count
        + slot_blocks[:, :, :, None] * BLOCK
        + offsets[None, None, None, :]
    ).reshape(-1)
    packed = jnp.take(patches.reshape(per_device * row_count, width), row_index, axis=0)
    packed = packed.reshape(group_size, capacity, -1, width)
    received = lax.all_to_all(packed, GY, split_axis=0, concat_axis=0, tiled=True)
    my_devices = jnp.take(device_of, my_column, axis=0)
    my_ranks = jnp.take(order_rank, my_column, axis=0)
    my_rows = received[my_devices, my_ranks].reshape(pairs_owned, 2, -1, width)
    gram = jnp.einsum(
        "pri,prj->pij", my_rows[:, 1], my_rows[:, 0], preferred_element_type=jnp.float32
    )
    rotation = newton_schulz(gram)
    q_ends = jnp.stack([jnp.swapaxes(rotation, 1, 2), rotation], axis=1).reshape(
        ends_count, width, width
    )
    device_numbers = jnp.arange(group_size, dtype=jnp.int32)
    placing = (
        (my_devices[None, None, :] == device_numbers[:, None, None])
        & (my_ranks[None, None, :] == slot_numbers[None, :, None])
    ).astype(jnp.float32)
    patch_numbers = jnp.arange(per_device, dtype=jnp.int32)
    slot_weights = (
        ((slot_patch[None] == patch_numbers[:, None, None]) & (slot_live[None] > 0))
        .astype(jnp.float32)
        .reshape(per_device, -1)
    )
    frames = newton_schulz(start_frames)
    rotation_slots = jnp.einsum("dce,eij->dcij", placing, q_ends, precision=lax.Precision.HIGHEST)
    rotation_recv = lax.all_to_all(
        rotation_slots, GY, split_axis=0, concat_axis=0, tiled=True
    ).reshape(-1, width, width)
    partner_flat = slot_partner.reshape(-1)
    for iteration in range(SWEEPS):
        frames_low = frames.astype(jnp.bfloat16)
        everyone = lax.all_gather(frames_low, GY, axis=0, tiled=True)
        partner = jnp.take(everyone, partner_flat, axis=0).astype(jnp.float32)
        estimate = jnp.einsum(
            "sij,sjk->sik", rotation_recv, partner, precision=lax.Precision.HIGHEST
        )
        summed = jnp.einsum("ps,sik->pik", slot_weights, estimate, precision=lax.Precision.HIGHEST)
        frames = newton_schulz(frames + summed)
    total_frame = sum_by_parts(jnp.sum(frames, axis=0), (("gx", "gy_0", "gy_1"), "gy_2"))
    gauge = newton_schulz(total_frame)
    final_frames = jnp.einsum("pij,kj->pik", frames, gauge, precision=lax.Precision.HIGHEST)
    aligned = jnp.einsum(
        "prd,pdk->prk",
        patches,
        final_frames.astype(jnp.bfloat16),
        preferred_element_type=jnp.float32,
    )
    return (aligned.astype(jnp.bfloat16), final_frames, total_frame)


def solution(mesh):
    torus = Mesh(mesh.devices.reshape(mesh.shape["gx"], 4, 4, 2), ("gx", "gy_0", "gy_1", "gy_2"))
    return jax.shard_map(
        local,
        mesh=torus,
        in_specs=(P(GX_GY, None, None), P(GX_GY, None, None), P("gx", None), P("gx", None, None)),
        out_specs=(P(GX_GY, None, None), P(GX_GY, None, None), P()),
        check_vma=False,
    )
```

profile of v0, /device:TPU:1, one launch (start us, length us, event | category | flops | bytes accessed | tf_op | source)
XLA Modules:
  0.0 567.2 jit_solution(18084156238551683727)
XLA Ops:
  7.2 0.7 rev.3
  9.0 0.9 copy.197
  11.0 63.5 %gather_fusion = bf16[16384,256]{1,0:T(8,128)(2,1)} fusion(bf16[8192,256]{1,0:T(8,128)(2,1)} %bitcast.206, s32[16384]{0:T(1024)S(1)} %broadcast_clamp_fusion), kind=kCustom, calls=%fused_computation.2 | custom fusion | bytes 16842752 | tf_op jit(solution)/shard_map/jit(_take)/gather | solution.py:115
  74.7 8.1 %broadcast_select_fusion = bf16[32,1,512,256]{3,2,1,0:T(8,128)(2,1)} fusion(bf16[32,1,512,256]{3,2,1,0:T(8,128)(2,1)} %bitcast.207, pred[32,512]{1,0:T(8,128)(4,1)S(1)} %compare_and_fusion), kind=kLoop, calls=%fused_computation.12 | loop fusion | flops 4194304 | bytes 16793600 | tf_op jit(solution)/shard_map/jit(_take)/select_n | solution.py:115
  82.8 9.6 %all-to-all-start = ((bf16[32,1,512,256]{3,2,1,0:T(8,128)(2,1)}), bf16[32,1,512,256]{3,2,1,0:T(8,128)(2,1)}, u32[]{:S(2)}, u32[]{:S(2)}) async-start(bf16[32,1,512,256]{3,2,1,0:T(8,128)(2,1)} %broadcast_select_fusion), calls=%async_computation | async-start | bytes 16777216 | tf_op jit(solution)/shard_map/all_to_all | solution.py:117
  92.9 0.8 fusion.95
  93.7 0.7 fusion.70
  94.4 0.8 convolution_add_fusion.14
  95.8 0.7 fusion.69
  97.8 0.7 fusion.68
  99.9 0.7 fusion.67
  101.9 0.7 fusion.66
  102.6 1.4 fusion.142
  104.4 94.2 %all-to-all-done = bf16[32,1,512,256]{3,2,1,0:T(8,128)(2,1)} async-done(((bf16[32,1,512,256]{3,2,1,0:T(8,128)(2,1)}), bf16[32,1,512,256]{3,2,1,0:T(8,128)(2,1)}, u32[]{:S(2)}, u32[]{:S(2)}) %all-to-all-start) | async-done | bytes 8388640 | tf_op jit(solution)/shard_map/all_to_all | solution.py:117
  198.6 6.6 %gather_fusion.1 = bf16[16,512,256]{2,1,0:T(8,128)(2,1)} fusion(bf16[32,1,512,256]{3,2,1,0:T(8,128)(2,1)} %all-to-all-done, s32[16]{0:T(128)S(1)} %fusion.125), kind=kCustom, calls=%fused_computation.3 | custom fusion | bytes 8388736 | tf_op jit(solution)/shard_map/gather | solution.py:120
  205.2 3.2 multiply_reduce_fusion
  208.4 2.8 fusion.48
  211.2 2.1 fusion.149
  213.4 2.6 multiply_add_fusion.4
  216.0 2.1 fusion.150
  218.1 2.1 fusion.151
  220.3 2.6 multiply_add_fusion.3
  222.9 2.1 fusion.152
  225.0 2.1 fusion.153
  227.1 2.4 multiply_add_fusion.2
  229.6 2.1 fusion.154
  231.7 2.5 fusion.155
  234.2 2.4 multiply_add_fusion.1
  236.7 2.1 fusion.156
  238.8 2.1 fusion.157
  240.9 2.4 multiply_add_fusion
  243.4 2.7 copy.201
  246.1 2.0 pad_maximum_fusion
  248.5 5.7 %fusion.15 = f32[32,1,256,256]{3,0,2,1:T(8,128)S(1)} fusion(f32[16,256,256]{2,1,0:T(8,128)S(1)} %bitcast.209, s32[16]{0:T(128)S(1)} %select_reduce_fusion.1, pred[16]{0:T(512)(128)(4,1)S(1)} %broadcast_compare_fusion.1), kind=kOutput, calls=%fused_computation.22 | convolution fusion | flops 402654208 | bytes 12582992 | tf_op jit(solution)/shard_map/dce,eij->dcij/dot_general | solution.py:140
  254.2 8.1 %copy.204 = f32[32,1,256,256]{3,2,1,0:T(8,128)} copy(f32[32,1,256,256]{3,0,2,1:T(8,128)S(1)} %fusion.15) | data formatting | bytes 16777216 | tf_op jit(solution)/shard_map/dce,eij->dcij/dot_general | solution.py:140
  262.3 20.2 %all-to-all-start.1 = ((f32[32,1,256,256]{3,2,1,0:T(8,128)}), f32[32,1,256,256]{3,2,1,0:T(8,128)}, u32[]{:S(2)}, u32[]{:S(2)}) async-start(f32[32,1,256,256]{3,2,1,0:T(8,128)} %copy.204), calls=%async_computation.1 | async-start | bytes 16777216 | tf_op jit(solution)/shard_map/all_to_all | solution.py:141
  282.6 6.2 %gather_fusion.2 = bf16[32,256,256]{2,1,0:T(8,128)(2,1)} fusion(bf16[64,256,256]{2,1,0:T(8,128)(2,1)} %all-gather.3.cloned.1.call-done, s32[1024]{0:T(1024)S(1)} %pad_clamp_fusion), kind=kCustom, calls=%fused_computation.clone | custom fusion | bytes 8388736 | tf_op jit(solution)/shard_map/jit(_take)/gather | solution.py:148
  288.8 94.4 %all-to-all-done.1 = f32[32,1,256,256]{3,2,1,0:T(8,128)} async-done(((f32[32,1,256,256]{3,2,1,0:T(8,128)}), f32[32,1,256,256]{3,2,1,0:T(8,128)}, u32[]{:S(2)}, u32[]{:S(2)}) %all-to-all-start.1) | async-done | bytes 8388640 | tf_op jit(solution)/shard_map/all_to_all | solution.py:141
  383.2 8.8 %fusion.2 = f32[32,256,256]{2,1,0:T(8,128)S(1)} fusion(f32[32,1,256,256]{3,2,1,0:T(8,128)} %all-to-all-done.1, bf16[32,256,256]{2,1,0:T(8,128)(2,1)} %gather_fusion.2, pred[32]{0:T(512)(128)(4,1)S(1)} %compare_and_fusion.1), kind=kOutput, calls=%fused_computation.6 | convolution fusion | flops 6444548096 | bytes 20971552 | tf_op jit(solution)/shard_map/sij,sjk->sik/dot_general | solution.py:149
  392.0 7.5 %fusion.6 = f32[2,256,256]{2,0,1:T(2,128)S(1)} fusion(f32[32,256,256]{2,1,0:T(8,128)S(1)} %fusion.2, pred[32]{0:T(512)(128)(4,1)S(1)} %broadcast_compare_fusion.2, s32[32]{0:T(128)S(1)} %get-tuple-element.45), kind=kOutput, calls=%fused_computation.10 | convolution fusion | flops 50331776 | bytes 8913056 | tf_op jit(solution)/shard_map/ps,sik->pik/dot_general | solution.py:152
  399.8 0.8 fusion.92
  400.6 0.7 fusion.65
  401.3 0.8 convolution_add_fusion.9
  402.7 0.7 fusion.64
  403.4 0.9 convolution_add_fusion.8
  404.9 0.7 fusion.63
  407.0 0.7 fusion.62
  409.0 0.7 fusion.61
  409.7 1.4 fusion.143
  411.1 55.6 %all-gather.5.cloned.1.call-done = bf16[64,256,256]{2,1,0:T(8,128)(2,1)} async-done(((bf16[2,256,256]{2,1,0:T(8,128)(2,1)}), bf16[64,256,256]{2,1,0:T(8,128)(2,1)}) %all-gather.5.cloned.1.call-update) | async-done | bytes 8388624 | tf_op jit(solution)/shard_map/all_gather | solution.py:147
  466.8 6.2 %gather_fusion.3 = bf16[32,256,256]{2,1,0:T(8,128)(2,1)} fusion(bf16[64,256,256]{2,1,0:T(8,128)(2,1)} %all-gather.5.cloned.1.call-done, s32[1024]{0:T(1024)S(1)} %pad_clamp_fusion), kind=kCustom, calls=%fused_computation.1.clone | custom fusion | bytes 8388736 | tf_op jit(solution)/shard_map/jit(_take)/gather | solution.py:148
  473.0 8.6 %fusion = f32[32,256,256]{2,1,0:T(8,128)S(1)} fusion(f32[32,1,256,256]{3,2,1,0:T(8,128)} %all-to-all-done.1, bf16[32,256,256]{2,1,0:T(8,128)(2,1)} %gather_fusion.3, pred[32]{0:T(512)(128)(4,1)S(1)} %compare_and_fusion.1), kind=kOutput, calls=%fused_computation.4 | convolution fusion | flops 6444548096 | bytes 20971552 | tf_op jit(solution)/shard_map/sij,sjk->sik/dot_general | solution.py:149
  481.6 7.5 %fusion.4 = f32[2,256,256]{2,0,1:T(2,128)S(1)} fusion(f32[32,256,256]{2,1,0:T(8,128)S(1)} %fusion, pred[32]{0:T(512)(128)(4,1)S(1)} %broadcast_compare_fusion.2, s32[32]{0:T(128)S(1)} %get-tuple-element.45), kind=kOutput, calls=%fused_computation.8 | convolution fusion | flops 50331776 | bytes 8913056 | tf_op jit(solution)/shard_map/ps,sik->pik/dot_general | solution.py:152
  489.4 0.8 fusion.89
  490.2 0.7 fusion.60
  490.9 0.8 convolution_add_fusion.4
  493.0 1.1 convolution_add_fusion.3
  498.8 0.7 fusion.56
  500.4 3.8 all_to_all.30
  504.5 16.8 %all_to_all.31 = f32[64,2,256]{2,1,0:T(2,128)S(1)} all-to-all(f32[64,2,256]{2,1,0:T(2,128)S(1)} %reduce_sum.127), channel_id=1, replica_groups=mesh['gx'=4,'gy_0'=4,'gy_1'=4,'gy_2'=2] {'gx','gy_0','gy_1'}, dimensions={0} | all-to-all | bytes 262144 | tf_op jit(solution)/shard_map/all_to_all | solution.py:57
  521.4 13.6 %all_to_all.32 = f32[64,2,256]{2,1,0:T(2,128)S(1)} all-to-all(f32[64,2,256]{2,1,0:T(2,128)S(1)} %broadcast_in_dim.34), channel_id=1, replica_groups=mesh['gx'=4,'gy_0'=4,'gy_1'=4,'gy_2'=2] {'gx','gy_0','gy_1'}, dimensions={0} | all-to-all | bytes 262144 | tf_op jit(solution)/shard_map/all_to_all | solution.py:24
  535.1 6.6 %all_to_all.33 = f32[2,64,2,256]{3,2,1,0:T(2,128)S(1)} all-to-all(f32[2,64,2,256]{3,2,1,0:T(2,128)S(1)} %broadcast_in_dim.35), channel_id=1, replica_groups=mesh['gx'=4,'gy_0'=4,'gy_1'=4,'gy_2'=2] {'gy_2'}, dimensions={0} | all-to-all | bytes 524288 | tf_op jit(solution)/shard_map/all_to_all | solution.py:24
  550.6 3.3 fusion.8
  553.9 6.3 %copy.217 = bf16[2,4096,256]{2,1,0:T(8,128)(2,1)} copy(bf16[2,4096,256]{1,2,0:T(8,128)(2,1)} %fusion.8) | data formatting | bytes 8388608
  (106 shorter events, 28.0 us)
Async XLA Ops:
  82.8 10.0 %copy-start.1 = (f32[2,256,256]{2,1,0:T(8,128)S(1)}, f32[2,256,256]{2,1,0:T(8,128)}, u32[]{:S(2)}) copy-start(f32[2,256,256]{2,1,0:T(8,128)} %param.9) | copy-start | bytes 1572868
  82.8 115.8 %all-to-all-start = ((bf16[32,1,512,256]{3,2,1,0:T(8,128)(2,1)}), bf16[32,1,512,256]{3,2,1,0:T(8,128)(2,1)}, u32[]{:S(2)}, u32[]{:S(2)}) async-start(bf16[32,1,512,256]{3,2,1,0:T(8,128)(2,1)} %broadcast_select_fusion), calls=%async_computation | async-start | bytes 16777216 | tf_op jit(solution)/shard_map/all_to_all | solution.py:117
  92.4 190.2 %all-gather.3.cloned.1.call-start = ((), (), s32[]{:S(2)}) async-start(), calls=%async_computation.6 | async-start | bytes 8650752 | tf_op jit(solution)/shard_map/all_gather | solution.py:147
  262.3 120.9 %all-to-all-start.1 = ((f32[32,1,256,256]{3,2,1,0:T(8,128)}), f32[32,1,256,256]{3,2,1,0:T(8,128)}, u32[]{:S(2)}, u32[]{:S(2)}) async-start(f32[32,1,256,256]{3,2,1,0:T(8,128)} %copy.204), calls=%async_computation.1 | async-start | bytes 16777216 | tf_op jit(solution)/shard_map/all_to_all | solution.py:141
  282.5 184.3 %all-gather.5.cloned.1.call-start = ((), (), s32[]{:S(2)}) async-start(), calls=%async_computation.7 | async-start | bytes 8650752 | tf_op jit(solution)/shard_map/all_gather | solution.py:147
  544.7 2.4 copy-start.3
  548.3 2.2 copy-start
  550.6 3.3 copy-start.2
Sparse Core Ops, SparseCore 0:
  104.2 109.6 all-gather.2
  411.3 55.4 all-gather.4
where the time goes:
time: 571 us; the launch traced here: 567 us
  waiting for transfers between devices  244 us (43%)
  matrix products  119 us (21%)
  local copies, waits for them, and re-layouts  104 us (18%)
  blocking collectives  40.8 us (7%)
  starting transfers between devices  30.1 us (5%)
  between operations  15.9 us (3%)
  other arithmetic  13.4 us (2%)
    all_to_all x1, waiting for transfers between devices, local(): lax.all_to_all(rotation_slots, GY, split_axis=0, concat_axis=0, tiled=True)  94.4 us
    all_to_all x1, waiting for transfers between devices, local(): lax.all_to_all(packed, GY, split_axis=0, concat_axis=0, tiled=True)  94.2 us
    gather x1, local copies, waits for them, and re-layouts, local(): jnp.take(patches.reshape(per_device * row_count, width), row_index, axis=0)  63.5 us
    all_gather x2, waiting for transfers between devices, local(): everyone = lax.all_gather(frames_low, GY, axis=0, tiled=True)  55.7 us
    dot_general x25, matrix products, newton_schulz(): jnp.einsum('...ij,...jk->...ik', polynom, matrix, precision=lax.Precision...  26.8 us
    dot_general x25, matrix products, newton_schulz(): jnp.einsum('...ij,...kj->...ik', matrix, matrix, precision=lax.Precision....  23.6 us
    dot_general x25, matrix products, newton_schulz(): jnp.einsum('...ij,...jk->...ik', square, square, precision=lax.Precision....  23.3 us
    all_to_all x2, blocking collectives, from_everyone(): lax.all_to_all(jnp.broadcast_to(value[None], (size, *value.shape)), axis,...  20.2 us
  transfers between devices with their start and end apart: 4, of which 3 were waited for; matrix products, arithmetic and copies ran while one was open for 14% of the time, Pallas kernels for 0%

commit v1 on v0

--- a/solution.py
+++ b/solution.py
@@ -144,7 +144,9 @@
     partner_flat = slot_partner.reshape(-1)
     for iteration in range(SWEEPS):
         frames_low = frames.astype(jnp.bfloat16)
-        everyone = lax.all_gather(frames_low, GY, axis=0, tiled=True)
+        everyone = jnp.concatenate(
+            lax.all_to_all(jnp.stack([frames_low] * lax.axis_size(GY)), GY, 0, 0), axis=0
+        )
         partner = jnp.take(everyone, partner_flat, axis=0).astype(jnp.float32)
         estimate = jnp.einsum(
             "sij,sjk->sik", rotation_recv, partner, precision=lax.Precision.HIGHEST

time: 571 us -> 643 us (1.13)
  blocking collectives: 40.8 us -> 146 us
  waiting for transfers between devices: 244 us -> 222 us
  between operations: 15.9 us -> 2.53 us
    all_to_all x0 -> x1, blocking collectives: none -> 105 us  [local(): lax.all_to_all(jnp.stack([frames_low] * lax.axis_size(GY)), GY, 0, 0)]
    all_gather x2 -> x0, waiting for transfers between devices: 55.7 us -> none  [local(): everyone = lax.all_gather(frames_low, GY, axis=0, tiled=True)]
    all_to_all x0 -> x1, waiting for transfers between devices: none -> 37.8 us  [local(): lax.all_to_all(jnp.stack([frames_low] * lax.axis_size(GY)), GY, 0, 0)]
    all_to_all x0 -> x1, starting transfers between devices: none -> 10.4 us  [local(): lax.all_to_all(jnp.stack([frames_low] * lax.axis_size(GY)), GY, 0, 0)]
    all_to_all x1, starting transfers between devices: 20.2 us -> 10.1 us  [local(): lax.all_to_all(rotation_slots, GY, split_axis=0, concat_axis=0, tiled=True)]
  transfers between devices with their start and end apart: 4 -> 3, of which waited for: 3 -> 3; matrix products, arithmetic and copies ran while one was open for 14% -> 12% of each run, Pallas kernels for 0% -> 0%
where the time goes in v1:
time: 643 us; the launch traced here: 640 us
  waiting for transfers between devices  222 us (35%)
  blocking collectives  146 us (23%)
  matrix products  117 us (18%)
  local copies, waits for them, and re-layouts  108 us (17%)
  starting transfers between devices  30.6 us (5%)
  other arithmetic  13.3 us (2%)
    all_to_all x1, blocking collectives, local(): lax.all_to_all(jnp.stack([frames_low] * lax.axis_size(GY)), GY, 0, 0)  105 us
    all_to_all x1, waiting for transfers between devices, local(): lax.all_to_all(rotation_slots, GY, split_axis=0, concat_axis=0, tiled=True)  94.4 us
    all_to_all x1, waiting for transfers between devices, local(): lax.all_to_all(packed, GY, split_axis=0, concat_axis=0, tiled=True)  90 us
    gather x1, local copies, waits for them, and re-layouts, local(): jnp.take(patches.reshape(per_device * row_count, width), row_index, axis=0)  63.5 us
    all_to_all x1, waiting for transfers between devices, local(): lax.all_to_all(jnp.stack([frames_low] * lax.axis_size(GY)), GY, 0, 0)  37.8 us
    dot_general x25, matrix products, newton_schulz(): jnp.einsum('...ij,...jk->...ik', polynom, matrix, precision=lax.Precision...  25.2 us
    dot_general x25, matrix products, newton_schulz(): jnp.einsum('...ij,...kj->...ik', matrix, matrix, precision=lax.Precision....  23.5 us
    dot_general x25, matrix products, newton_schulz(): jnp.einsum('...ij,...jk->...ik', square, square, precision=lax.Precision....  23 us
  transfers between devices with their start and end apart: 3, of which 3 were waited for; matrix products, arithmetic and copies ran while one was open for 12% of the time, Pallas kernels for 0%

profile of v1, /device:TPU:1, one launch (start us, length us, event | category | flops | bytes accessed | tf_op | source)
XLA Modules:
  0.0 639.6 jit_solution(5391340658357652676)
XLA Ops:
  0.7 0.7 rev.3
  3.2 0.9 copy.197
  4.7 63.5 %gather_fusion = bf16[16384,256]{1,0:T(8,128)(2,1)} fusion(bf16[8192,256]{1,0:T(8,128)(2,1)} %bitcast.208, s32[16384]{0:T(1024)S(1)} %broadcast_clamp_fusion), kind=kCustom, calls=%fused_computation.2 | custom fusion | bytes 16842752 | tf_op jit(solution)/shard_map/jit(_take)/gather | solution.py:115
  68.2 8.0 %broadcast_select_fusion = bf16[32,1,512,256]{3,2,1,0:T(8,128)(2,1)} fusion(bf16[32,1,512,256]{3,2,1,0:T(8,128)(2,1)} %bitcast.209, pred[32,512]{1,0:T(8,128)(4,1)S(1)} %compare_and_fusion), kind=kLoop, calls=%fused_computation.12 | loop fusion | flops 4194304 | bytes 16793600 | tf_op jit(solution)/shard_map/jit(_take)/select_n | solution.py:115
  76.2 10.1 %all-to-all-start = ((bf16[32,1,512,256]{3,2,1,0:T(8,128)(2,1)}), bf16[32,1,512,256]{3,2,1,0:T(8,128)(2,1)}, u32[]{:S(2)}, u32[]{:S(2)}) async-start(bf16[32,1,512,256]{3,2,1,0:T(8,128)(2,1)} %broadcast_select_fusion), calls=%async_computation | async-start | bytes 16777216 | tf_op jit(solution)/shard_map/all_to_all | solution.py:117
  86.5 0.8 fusion.95
  87.3 0.7 fusion.70
  88.0 0.8 convolution_add_fusion.14
  89.4 0.7 fusion.69
  91.5 0.7 fusion.68
  93.5 0.7 fusion.67
  95.5 0.7 fusion.66
  96.9 90.0 %all-to-all-done = bf16[32,1,512,256]{3,2,1,0:T(8,128)(2,1)} async-done(((bf16[32,1,512,256]{3,2,1,0:T(8,128)(2,1)}), bf16[32,1,512,256]{3,2,1,0:T(8,128)(2,1)}, u32[]{:S(2)}, u32[]{:S(2)}) %all-to-all-start) | async-done | bytes 8388640 | tf_op jit(solution)/shard_map/all_to_all | solution.py:117
  187.0 4.2 stack.13
  191.2 10.4 %all-to-all-start.2 = ((bf16[32,2,256,256]{3,2,1,0:T(8,128)(2,1)}), bf16[32,2,256,256]{3,2,1,0:T(8,128)(2,1)}, u32[]{:S(2)}, u32[]{:S(2)}) async-start(bf16[32,2,256,256]{3,2,1,0:T(8,128)(2,1)} %stack.13), calls=%async_computation.2 | async-start | bytes 16777216 | tf_op jit(solution)/shard_map/all_to_all | solution.py:148
  202.0 6.2 gather_fusion.1
  208.2 3.1 multiply_reduce_fusion
  211.3 2.3 fusion.48
  213.6 2.1 fusion.149
  215.8 2.6 multiply_add_fusion.4
  218.4 2.1 fusion.150
  220.5 2.3 fusion.151
  222.9 2.4 multiply_add_fusion.3
  225.3 2.1 fusion.152
  227.4 2.1 fusion.153
  229.6 2.4 multiply_add_fusion.2
  232.0 2.5 fusion.154
  234.5 2.1 fusion.155
  236.7 2.4 multiply_add_fusion.1
  239.1 2.1 fusion.156
  241.2 2.1 fusion.157
  243.3 2.4 multiply_add_fusion
  245.8 2.0 copy.201
  247.7 2.0 pad_maximum_fusion
  250.1 5.7 fusion.15
  255.9 8.1 %copy.204 = f32[32,1,256,256]{3,2,1,0:T(8,128)} copy(f32[32,1,256,256]{3,0,2,1:T(8,128)S(1)} %fusion.15) | data formatting | bytes 16777216 | tf_op jit(solution)/shard_map/dce,eij->dcij/dot_general | solution.py:140
  263.9 37.8 %all-to-all-done.2 = bf16[32,2,256,256]{3,2,1,0:T(8,128)(2,1)} async-done(((bf16[32,2,256,256]{3,2,1,0:T(8,128)(2,1)}), bf16[32,2,256,256]{3,2,1,0:T(8,128)(2,1)}, u32[]{:S(2)}, u32[]{:S(2)}) %all-to-all-start.2) | async-done | bytes 8388640 | tf_op jit(solution)/shard_map/all_to_all | solution.py:148
  301.8 10.1 %all-to-all-start.1 = ((f32[32,1,256,256]{3,2,1,0:T(8,128)}), f32[32,1,256,256]{3,2,1,0:T(8,128)}, u32[]{:S(2)}, u32[]{:S(2)}) async-start(f32[32,1,256,256]{3,2,1,0:T(8,128)} %copy.204), calls=%async_computation.1 | async-start | bytes 16777216 | tf_op jit(solution)/shard_map/all_to_all | solution.py:141
  312.0 6.2 gather_fusion.2
  318.2 94.4 %all-to-all-done.1 = f32[32,1,256,256]{3,2,1,0:T(8,128)} async-done(((f32[32,1,256,256]{3,2,1,0:T(8,128)}), f32[32,1,256,256]{3,2,1,0:T(8,128)}, u32[]{:S(2)}, u32[]{:S(2)}) %all-to-all-start.1) | async-done | bytes 8388640 | tf_op jit(solution)/shard_map/all_to_all | solution.py:141
  412.6 8.8 %fusion.2 = f32[32,256,256]{2,1,0:T(8,128)S(1)} fusion(f32[32,1,256,256]{3,2,1,0:T(8,128)} %all-to-all-done.1, bf16[32,256,256]{2,1,0:T(8,128)(2,1)} %gather_fusion.2, pred[32]{0:T(512)(128)(4,1)S(1)} %compare_and_fusion.1), kind=kOutput, calls=%fused_computation.6 | convolution fusion | flops 6444548096 | bytes 20971552 | tf_op jit(solution)/shard_map/sij,sjk->sik/dot_general | solution.py:151
  421.5 7.5 %fusion.6 = f32[2,256,256]{2,0,1:T(2,128)S(1)} fusion(f32[32,256,256]{2,1,0:T(8,128)S(1)} %fusion.2, pred[32]{0:T(512)(128)(4,1)S(1)} %broadcast_compare_fusion.2, s32[32]{0:T(128)S(1)} %get-tuple-element.45), kind=kOutput, calls=%fused_computation.10 | convolution fusion | flops 50331776 | bytes 8913056 | tf_op jit(solution)/shard_map/ps,sik->pik/dot_general | solution.py:154
  429.2 0.8 fusion.92
  430.0 0.7 fusion.65
  430.7 0.8 convolution_add_fusion.9
  432.1 0.7 fusion.64
  432.8 0.9 convolution_add_fusion.8
  434.3 0.7 fusion.63
  438.4 0.7 fusion.61
  439.8 1.0 stack.14
  440.8 104.8 %all_to_all.40 = bf16[32,2,256,256]{3,2,1,0:T(8,128)(2,1)} all-to-all(bf16[32,2,256,256]{3,2,1,0:T(8,128)(2,1)S(1)} %stack.14), channel_id=1, replica_groups=mesh['gx'=4,'gy_0'=4,'gy_1'=4,'gy_2'=2] {'gy_0','gy_1','gy_2'}, dimensions={0} | all-to-all | bytes 16777216 | tf_op jit(solution)/shard_map/all_to_all | solution.py:148
  545.7 6.2 gather_fusion.3
  551.9 8.6 %fusion = f32[32,256,256]{2,1,0:T(8,128)S(1)} fusion(f32[32,1,256,256]{3,2,1,0:T(8,128)} %all-to-all-done.1, bf16[32,256,256]{2,1,0:T(8,128)(2,1)} %gather_fusion.3, pred[32]{0:T(512)(128)(4,1)S(1)} %compare_and_fusion.1), kind=kOutput, calls=%fused_computation.4 | convolution fusion | flops 6444548096 | bytes 20971552 | tf_op jit(solution)/shard_map/sij,sjk->sik/dot_general | solution.py:151
  560.5 7.5 %fusion.4 = f32[2,256,256]{2,0,1:T(2,128)S(1)} fusion(f32[32,256,256]{2,1,0:T(8,128)S(1)} %fusion, pred[32]{0:T(512)(128)(4,1)S(1)} %broadcast_compare_fusion.2, s32[32]{0:T(128)S(1)} %get-tuple-element.45), kind=kOutput, calls=%fused_computation.8 | convolution fusion | flops 50331776 | bytes 8913056 | tf_op jit(solution)/shard_map/ps,sik->pik/dot_general | solution.py:154
  568.3 0.8 fusion.89
  569.7 0.8 convolution_add_fusion.4
  571.2 0.7 fusion.59
  571.9 1.1 convolution_add_fusion.3
  579.3 4.0 all_to_all.41
  583.5 17.0 %all_to_all.42 = f32[64,2,256]{2,1,0:T(2,128)S(1)} all-to-all(f32[64,2,256]{2,1,0:T(2,128)S(1)} %reduce_sum.127), channel_id=1, replica_groups=mesh['gx'=4,'gy_0'=4,'gy_1'=4,'gy_2'=2] {'gx','gy_0','gy_1'}, dimensions={0} | all-to-all | bytes 262144 | tf_op jit(solution)/shard_map/all_to_all | solution.py:57
  600.6 13.6 %all_to_all.43 = f32[64,2,256]{2,1,0:T(2,128)S(1)} all-to-all(f32[64,2,256]{2,1,0:T(2,128)S(1)} %broadcast_in_dim.34), channel_id=1, replica_groups=mesh['gx'=4,'gy_0'=4,'gy_1'=4,'gy_2'=2] {'gx','gy_0','gy_1'}, dimensions={0} | all-to-all | bytes 262144 | tf_op jit(solution)/shard_map/all_to_all | solution.py:24
  614.3 6.6 %all_to_all.44 = f32[2,64,2,256]{3,2,1,0:T(2,128)S(1)} all-to-all(f32[2,64,2,256]{3,2,1,0:T(2,128)S(1)} %broadcast_in_dim.35), channel_id=1, replica_groups=mesh['gx'=4,'gy_0'=4,'gy_1'=4,'gy_2'=2] {'gy_2'}, dimensions={0} | all-to-all | bytes 524288 | tf_op jit(solution)/shard_map/all_to_all | solution.py:24
  629.8 3.3 fusion.8
  633.1 6.3 copy.217
  (105 shorter events, 30.3 us)
Async XLA Ops:
  76.2 10.1 %copy-start.1 = (f32[2,256,256]{2,1,0:T(8,128)S(1)}, f32[2,256,256]{2,1,0:T(8,128)}, u32[]{:S(2)}) copy-start(f32[2,256,256]{2,1,0:T(8,128)} %param.9) | copy-start | bytes 1572868
  76.2 110.7 %all-to-all-start = ((bf16[32,1,512,256]{3,2,1,0:T(8,128)(2,1)}), bf16[32,1,512,256]{3,2,1,0:T(8,128)(2,1)}, u32[]{:S(2)}, u32[]{:S(2)}) async-start(bf16[32,1,512,256]{3,2,1,0:T(8,128)(2,1)} %broadcast_select_fusion), calls=%async_computation | async-start | bytes 16777216 | tf_op jit(solution)/shard_map/all_to_all | solution.py:117
  191.2 110.6 %all-to-all-start.2 = ((bf16[32,2,256,256]{3,2,1,0:T(8,128)(2,1)}), bf16[32,2,256,256]{3,2,1,0:T(8,128)(2,1)}, u32[]{:S(2)}, u32[]{:S(2)}) async-start(bf16[32,2,256,256]{3,2,1,0:T(8,128)(2,1)} %stack.13), calls=%async_computation.2 | async-start | bytes 16777216 | tf_op jit(solution)/shard_map/all_to_all | solution.py:148
  301.8 110.9 %all-to-all-start.1 = ((f32[32,1,256,256]{3,2,1,0:T(8,128)}), f32[32,1,256,256]{3,2,1,0:T(8,128)}, u32[]{:S(2)}, u32[]{:S(2)}) async-start(f32[32,1,256,256]{3,2,1,0:T(8,128)} %copy.204), calls=%async_computation.1 | async-start | bytes 16777216 | tf_op jit(solution)/shard_map/all_to_all | solution.py:141
  622.7 2.1 copy-start.3
  627.5 2.2 copy-start
  629.7 3.3 copy-start.2
